TPU v7x, 32 devices: a whole 2x2x4 slice. The times are simulated.
32 devices in a mesh: sample: 4 (over z), tensor: 2 (over y), section: 4 (over x, core).
Axes of the slice: x: 2, y: 2, z: 4, core: 2. Of those that a mesh axis runs over, the one named last changes fastest.
Arguments:
- hidden_in: bfloat16 [512, 8192], P('sample', 'section'), may hold values from -6 to 6
- token_ids: int32 [512], P('sample'), may hold values from 0 to 128255, as said below
- mlp_gain: bfloat16 [8192], P('section'), may hold values from 0.099609375 to 1.8984375
- attn_gain: bfloat16 [8192], P('section'), may hold values from 0.099609375 to 1.8984375
- gate_weight: bfloat16 [28672, 8192], P(('sample', 'tensor'), 'section'), may hold values from -0.0625 to 0.0625
- up_weight: bfloat16 [28672, 8192], P(('sample', 'tensor'), 'section'), may hold values from -0.0625 to 0.0625
- down_weight: bfloat16 [28672, 8192], P(('sample', 'tensor'), 'section'), may hold values from -0.03125 to 0.03125
Outputs:
- hidden_out: bfloat16 [512, 8192], P('sample', 'section')
- mlp_cov: float32 [8192, 8192], P('section', ('sample', 'tensor'))
- attn_cov: float32 [8192, 8192], P('section', ('sample', 'tensor'))
Inputs may be any that keep to these rules, and one draw needn't show every extreme that they name: `token_ids`: 0 is padding and is left out of the statistics; within each block of 128 rows the padding forms the tail, and the last block has none.
All inputs are finite; a program needn't handle non-finite values.
Results may differ from a plain program's by a relative error of at most 0.0071.
Values may be sent and summed in bfloat16 or wider, within the bound.
A program may use at most 256 MiB of HBM per device.

v0:
```python
import jax
import jax.numpy as jnp
from jax import lax
from jax.sharding import PartitionSpec as P

D = 8192
EPS = 1e-05
ROW_CONTRACT = (((1,), (1,)), ((), ()))
TOKEN_CONTRACT = (((0,), (0,)), ((), ()))


def broadcast(block, axis, source):
    block = jnp.where(lax.axis_index(axis) == source, block, jnp.zeros_like(block))
    return lax.psum(block, axis)


def rms_norm(values, totals, gain):
    scales = lax.rsqrt(totals / D + EPS)
    return (values * scales[:, None] * gain.astype(jnp.float32)).astype(jnp.bfloat16)


def covariance(rows_in, columns, live_mask, live_count):
    weighted = rows_in * live_mask[:, None]
    products = lax.dot_general(
        weighted, columns, TOKEN_CONTRACT, preferred_element_type=jnp.float32
    )
    row_means = jnp.dot(live_mask, rows_in, preferred_element_type=jnp.float32) / live_count
    col_means = jnp.dot(live_mask, columns, preferred_element_type=jnp.float32) / live_count
    return products / live_count - row_means[:, None] * col_means[None, :]


def local(hidden_in, token_ids, mlp_gain, attn_gain, gate_weight, up_weight, down_weight):
    n_sample = lax.axis_size("sample")
    n_tensor = lax.axis_size("tensor")
    panel = hidden_in.shape[1]
    tok_local = hidden_in.shape[0]
    col_width = D // (n_sample * n_tensor)
    column_index = lax.axis_index("sample") * n_tensor + lax.axis_index("tensor")
    owner_section = column_index * col_width // panel
    column_start = column_index * col_width - owner_section * panel
    values = hidden_in.astype(jnp.float32)
    totals = lax.psum(jnp.sum(values * values, axis=1), "section")
    mlp_input = rms_norm(values, totals, mlp_gain)
    live_local = (token_ids != 0).astype(jnp.bfloat16)
    rows_in, mask_rows = lax.all_gather((mlp_input, live_local), "sample", axis=0, tiled=True)
    gate_part = lax.dot_general(
        rows_in, gate_weight, ROW_CONTRACT, preferred_element_type=jnp.float32
    )
    up_part = lax.dot_general(rows_in, up_weight, ROW_CONTRACT, preferred_element_type=jnp.float32)
    mlp_rows, live_mask, gate_part, up_part = (rows_in, mask_rows, gate_part, up_part)
    live_count = jnp.sum(live_mask.astype(jnp.float32))
    gate_share, up_share = (
        lax.psum_scatter(gate_part, "section", scatter_dimension=0, tiled=True),
        lax.psum_scatter(up_part, "section", scatter_dimension=0, tiled=True),
    )
    share_units = (jax.nn.silu(gate_share) * up_share).astype(jnp.bfloat16)
    hidden_units = lax.all_gather(share_units, "section", axis=0, tiled=True)
    share_rows = tok_local // n_tensor
    residual = lax.psum_scatter(
        jnp.dot(hidden_units, down_weight, preferred_element_type=jnp.float32),
        ("sample", "tensor"),
        scatter_dimension=0,
        tiled=True,
    )
    own_rows = lax.dynamic_slice_in_dim(
        values, lax.axis_index("tensor") * share_rows, share_rows, 0
    )
    updated = (own_rows + residual).astype(jnp.bfloat16)
    hidden_out = lax.all_gather(updated, "tensor", axis=0, tiled=True)
    out_values = hidden_out.astype(jnp.float32)
    out_totals = lax.psum(jnp.sum(out_values * out_values, axis=1), "section")
    attn_input = rms_norm(out_values, out_totals, attn_gain)
    mlp_pick = lax.dynamic_slice_in_dim(mlp_rows, column_start, col_width, 1)
    mlp_columns = broadcast(mlp_pick, "section", owner_section)
    mlp_cov = covariance(mlp_rows, mlp_columns, live_mask, live_count)
    attn_rows = lax.all_gather(attn_input, "sample", axis=0, tiled=True)
    attn_pick = lax.dynamic_slice_in_dim(attn_rows, column_start, col_width, 1)
    attn_columns = broadcast(attn_pick, "section", owner_section)
    attn_cov = covariance(attn_rows, attn_columns, live_mask, live_count)
    return (hidden_out, mlp_cov, attn_cov)


def solution(mesh):
    in_specs = (
        P("sample", "section"),
        P("sample"),
        P("section"),
        P("section"),
        P(("sample", "tensor"), "section"),
        P(("sample", "tensor"), "section"),
        P(("sample", "tensor"), "section"),
    )
    out_specs = (
        P("sample", "section"),
        P("section", ("sample", "tensor")),
        P("section", ("sample", "tensor")),
    )
    return jax.shard_map(local, mesh=mesh, in_specs=in_specs, out_specs=out_specs, check_vma=False)
```

profile of v0, /device:TPU:0, one launch (start us, length us, event | category | flops | bytes accessed | tf_op | source)
XLA Modules:
  0.0 492.0 jit_solution(1465766490819151199)
XLA Ops:
  7.2 0.0 all-gather.5.cloned.1.call-start
  7.2 1.2 multiply_reduce_fusion
  8.4 8.4 %psum.28 = f32[128]{0:T(128)S(1)} all-reduce(f32[128]{0:T(128)S(1)} %multiply_reduce_fusion), channel_id=1, replica_groups=mesh['sample'=4,'tensor'=2,'section'=4] {'section'}, use_global_device_ids=true, to_apply=%region_1.2 | all-reduce | flops 128 | bytes 1024 | tf_op jit(solution)/shard_map/psum | solution.py:42
  16.8 0.7 convert_element_type.31
  17.5 2.0 multiply_convert_fusion.1
  19.5 0.0 all-gather.5.cloned.1.call-update
  19.6 0.0 reduce-scatter.6.cloned.1.call-start
  19.6 46.1 %all-gather.5.cloned.1.call-done = bf16[512,2048]{1,0:T(8,128)(2,1)} async-done(((bf16[128,2048]{1,0:T(8,128)(2,1)}), bf16[512,2048]{1,0:T(8,128)(2,1)}) %all-gather.5.cloned.1.call-update) | async-done | bytes 2097168 | tf_op jit(solution)/shard_map/all_gather | solution.py:45
  65.7 13.5 %fusion.17 = f32[512,3584]{1,0:T(8,128)} fusion(bf16[512,2048]{1,0:T(8,128)(2,1)} %all-gather.5.cloned.1.call-done, bf16[3584,2048]{1,0:T(8,128)(2,1)} %param.12), kind=kOutput, calls=%fused_computation.35 | convolution fusion | flops 7516192768 | bytes 24117248 | tf_op jit(solution)/shard_map/dot_general | solution.py:49
  79.2 0.0 copy-start.1
  79.2 0.0 reduce-scatter.6.cloned.1.call-update
  79.2 0.0 reduce-scatter.4.cloned.1.call-start
  79.3 1.5 copy-done.1
  80.8 13.3 %fusion.16 = f32[512,3584]{1,0:T(8,128)} fusion(bf16[512,2048]{1,0:T(8,128)(2,1)S(1)} %copy-done.1, bf16[3584,2048]{1,0:T(8,128)(2,1)} %param.11), kind=kOutput, calls=%fused_computation.34 | convolution fusion | flops 7516192768 | bytes 24117248 | tf_op jit(solution)/shard_map/dot_general | solution.py:46
  94.1 0.0 reduce-scatter.4.cloned.1.call-update
  94.1 0.0 all-gather.7.cloned.1.call-start
  94.2 50.0 %reduce-scatter.6.cloned.1.call-done = f32[128,3584]{1,0:T(8,128)} async-done(((f32[512,3584]{1,0:T(8,128)}), f32[128,3584]{1,0:T(8,128)}) %reduce-scatter.6.cloned.1.call-update) | async-done | bytes 1835024 | tf_op jit(solution)/shard_map/reduce_scatter | solution.py:54
  144.2 69.1 %reduce-scatter.4.cloned.1.call-done = f32[128,3584]{1,0:T(8,128)} async-done(((f32[512,3584]{1,0:T(8,128)}), f32[128,3584]{1,0:T(8,128)}) %reduce-scatter.4.cloned.1.call-update) | async-done | bytes 1835024 | tf_op jit(solution)/shard_map/reduce_scatter | solution.py:53
  213.3 3.5 multiply_convert_fusion
  216.7 0.0 all-gather.7.cloned.1.call-update
  216.8 0.0 reduce-scatter.8.cloned.1.call-start
  216.8 31.6 %all-gather.7.cloned.1.call-done = bf16[512,3584]{1,0:T(8,128)(2,1)} async-done(((bf16[128,3584]{1,0:T(8,128)(2,1)}), bf16[512,3584]{1,0:T(8,128)(2,1)}) %all-gather.7.cloned.1.call-update) | async-done | bytes 3670032 | tf_op jit(solution)/shard_map/all_gather | solution.py:57
  248.4 13.4 %fusion.18 = f32[512,2048]{1,0:T(8,128)} fusion(bf16[512,3584]{1,0:T(8,128)(2,1)} %all-gather.7.cloned.1.call-done, bf16[3584,2048]{1,0:T(8,128)(2,1)} %param.13), kind=kOutput, calls=%fused_computation.36 | convolution fusion | flops 7516192768 | bytes 22544384 | tf_op jit(solution)/shard_map/dot_general | solution.py:60
  261.7 0.0 copy-start
  261.7 0.0 copy-start.3
  261.7 0.0 reduce-scatter.8.cloned.1.call-update
  261.8 0.0 copy-start.4
  261.8 0.0 all-gather.9.cloned.1.call-start
  261.8 0.9 copy-done
  262.8 1.1 convert_element_type.30
  263.9 0.0 copy-done.3
  263.9 86.8 %reduce-scatter.8.cloned.1.call-done = f32[64,2048]{1,0:T(8,128)} async-done(((f32[512,2048]{1,0:T(8,128)}), f32[64,2048]{1,0:T(8,128)}) %reduce-scatter.8.cloned.1.call-update) | async-done | bytes 524304 | tf_op jit(solution)/shard_map/reduce_scatter | solution.py:59
  350.6 1.3 add_convert_fusion
  351.9 8.3 %all_gather.17 = bf16[128,2048]{1,0:T(8,128)(2,1)S(1)} all-gather(bf16[64,2048]{1,0:T(8,128)(2,1)S(1)} %add_convert_fusion), channel_id=1, replica_groups=mesh['sample'=4,'tensor'=2,'section'=4] {'tensor'}, dimensions={0}, use_global_device_ids=true | all-gather | bytes 786432 | tf_op jit(solution)/shard_map/all_gather | solution.py:69
  360.2 0.2 fusion.2
  360.4 5.7 %psum.30 = f32[128]{0:T(128)S(1)} all-reduce(f32[128]{0:T(128)S(1)} %fusion.2), channel_id=1, replica_groups=mesh['sample'=4,'tensor'=2,'section'=4] {'section'}, use_global_device_ids=true, to_apply=%region_8.9 | all-reduce | flops 128 | bytes 1024 | tf_op jit(solution)/shard_map/psum | solution.py:71
  366.1 1.0 fusion.4
  367.0 0.0 all-gather.9.cloned.1.call-update
  367.1 0.0 all-reduce.3.cloned.1.call-start
  367.1 0.0 copy-done.4
  367.2 10.6 %all-gather = bf16[4,1,128]{2,1,0:T(2,128)(2,1)S(1)} all-gather(bf16[1,1,128]{2,1,0:T(2,128)(2,1)S(1)} %fusion.15), channel_id=1, replica_groups=mesh['sample'=4,'tensor'=2,'section'=4] {'sample'}, dimensions={0}, use_global_device_ids=true | all-gather | bytes 1280 | tf_op jit(solution)/shard_map/all_gather | solution.py:45
  377.8 1.2 dynamic-slice_select_fusion.1
  379.0 34.4 %all-gather.9.cloned.1.call-done = bf16[512,2048]{1,0:T(8,128)(2,1)} async-done(((bf16[128,2048]{1,0:T(8,128)(2,1)}), bf16[512,2048]{1,0:T(8,128)(2,1)}) %all-gather.9.cloned.1.call-update) | async-done | bytes 2097168 | tf_op jit(solution)/shard_map/all_gather | solution.py:76
  413.4 2.4 dynamic-slice_select_fusion
  415.8 0.0 all-reduce.3.cloned.1.call-update
  415.8 0.6 convert_reduce_fusion
  416.4 0.4 fusion.13
  416.8 0.7 broadcast_divide_fusion.1
  417.5 2.0 fusion.9
  419.4 0.7 broadcast_divide_fusion
  420.1 46.5 %all-reduce.3.cloned.1.call-done = (bf16[512,1024]{1,0:T(8,128)(2,1)}, bf16[512,1024]{1,0:T(8,128)(2,1)}) async-done(((bf16[512,1024]{1,0:T(8,128)(2,1)}, bf16[512,1024]{1,0:T(8,128)(2,1)}), (bf16[512,1024]{1,0:T(8,128)(2,1)}, bf16[512,1024]{1,0:T(8,128)(2,1)})) %all-reduce.3.cloned.1.call-update) | async-done | bytes 2097168 | tf_op jit(solution)/shard_map/psum | solution.py:14
  466.6 1.5 fusion.11
  468.1 1.5 fusion.7
  469.6 0.7 broadcast_divide_fusion.2
  470.3 0.0 copy-start.2
  470.3 8.6 %multiply_subtract_fusion = f32[2048,1024]{1,0:T(8,128)} fusion(f32[1024]{0:T(1024)S(1)} %get-tuple-element.5, f32[2048]{0:T(1024)S(1)} %broadcast_divide_fusion, f32[]{:T(128)} %convert_reduce_fusion, bf16[512,1024]{1,0:T(8,128)(2,1)} %get-tuple-element.4, bf16[512,2048]{1,0:T(8,128)(2,1)} %all-gather.9.cloned.1.call-done, bf16[512]{0:T(512)(128)(2,1)S(1)} %bitcast.33), kind=kOutput, calls=%fused_computation | convolution fusion | flops 2154823680 | bytes 11547652 | tf_op jit(solution)/shard_map/dot_general | solution.py:24
  478.9 0.0 copy-done.2
  478.9 5.5 %multiply_subtract_fusion.1 = f32[2048,1024]{1,0:T(8,128)} fusion(f32[1024]{0:T(1024)S(1)} %get-tuple-element.6, f32[2048]{0:T(1024)S(1)} %broadcast_divide_fusion.1, f32[]{:T(128)} %convert_reduce_fusion, bf16[512,1024]{1,0:T(8,128)(2,1)S(1)} %copy-done.2, bf16[512,2048]{1,0:T(8,128)(2,1)S(1)} %copy-done.1, bf16[512]{0:T(512)(128)(2,1)S(1)} %bitcast.34), kind=kOutput, calls=%fused_computation.1 | convolution fusion | flops 2154823680 | bytes 11547652 | tf_op jit(solution)/shard_map/dot_general | solution.py:24
  484.4 0.8 copy.13
  (5 shorter events, 0.0 us)
Async XLA Ops:
  7.2 58.5 %all-gather.5.cloned.1.call-start = ((), (), s32[]{:S(2)}) async-start(), calls=%async_computation.3 | async-start | bytes 2621440 | tf_op jit(solution)/shard_map/all_gather | solution.py:45
  19.6 124.6 %reduce-scatter.6.cloned.1.call-start = ((), (), s32[]{:S(2)}) async-start(), calls=%async_computation.5 | async-start | bytes 9175040 | tf_op jit(solution)/shard_map/reduce_scatter | solution.py:54
  79.2 1.6 copy-start.1
  79.2 134.0 %reduce-scatter.4.cloned.1.call-start = ((), (), s32[]{:S(2)}) async-start(), calls=%async_computation.4 | async-start | bytes 9175040 | tf_op jit(solution)/shard_map/reduce_scatter | solution.py:53
  94.1 154.3 %all-gather.7.cloned.1.call-start = ((), (), s32[]{:S(2)}) async-start(), calls=%async_computation.6 | async-start | bytes 4587520 | tf_op jit(solution)/shard_map/all_gather | solution.py:57
  216.8 133.9 %reduce-scatter.8.cloned.1.call-start = ((), (), s32[]{:S(2)}) async-start(), calls=%async_computation.7 | async-start | bytes 4718592 | tf_op jit(solution)/shard_map/reduce_scatter | solution.py:59
  261.7 1.0 copy-start
  261.7 2.1 copy-start.3
  261.8 105.4 %copy-start.4 = (s32[128]{0:T(128)S(1)}, s32[128]{0:T(128)}, u32[]{:S(2)}) copy-start(s32[128]{0:T(128)} %param.8) | copy-start | bytes 1540
  261.8 151.6 %all-gather.9.cloned.1.call-start = ((), (), s32[]{:S(2)}) async-start(), calls=%async_computation.8 | async-start | bytes 2621440 | tf_op jit(solution)/shard_map/all_gather | solution.py:76
  367.1 99.6 %all-reduce.3.cloned.1.call-start = ((), (), s32[]{:S(2)}) async-start(), calls=%async_computation.9 | async-start | bytes 4194304 | tf_op jit(solution)/shard_map/psum | solution.py:14
  470.3 8.6 %copy-start.2 = (bf16[512,1024]{1,0:T(8,128)(2,1)S(1)}, bf16[512,1024]{1,0:T(8,128)(2,1)}, u32[]{:S(2)}) copy-start(bf16[512,1024]{1,0:T(8,128)(2,1)} %get-tuple-element.3) | copy-start | bytes 3145732
Sparse Core Ops, SparseCore 0:
  19.7 45.9 all-gather.4
  79.4 64.7 reduce-scatter.5
  147.3 65.9 reduce-scatter.3
  216.9 31.4 all-gather.6
  261.9 88.6 reduce-scatter.7
  367.2 46.1 all-gather.8
  416.4 50.1 all-reduce.2
where the time goes:
time: 493 us; the launch traced here: 492 us
  waiting for transfers between devices  365 us (74%)
  matrix products  59.6 us (12%)
  blocking collectives  33 us (7%)
  other arithmetic  17.1 us (3%)
  between operations  14.2 us (3%)
    reduce_scatter x1, waiting for transfers between devices, local(): lax.psum_scatter(jnp.dot(hidden_units, down_weight, preferred_element_typ...  86.8 us
    reduce_scatter x1, waiting for transfers between devices, local(): lax.psum_scatter(gate_part, 'section', scatter_dimension=0, tiled=True)  69.1 us
    reduce_scatter x1, waiting for transfers between devices, local(): lax.psum_scatter(up_part, 'section', scatter_dimension=0, tiled=True)  50 us
    psum x1, waiting for transfers between devices, broadcast(): return lax.psum(block, axis)  46.5 us
    all_gather x1, waiting for transfers between devices, local(): lax.all_gather((mlp_input, live_local), 'sample', axis=0, tiled=True)  46.1 us
    all_gather x1, waiting for transfers between devices, local(): attn_rows = lax.all_gather(attn_input, 'sample', axis=0, tiled=True)  34.4 us
    all_gather x1, waiting for transfers between devices, local(): hidden_units = lax.all_gather(share_units, 'section', axis=0, tiled=True)  31.6 us
    dot_general x2, matrix products, covariance(): lax.dot_general(weighted, columns, TOKEN_CONTRACT, preferred_element_type...  14.1 us
  transfers between devices with their start and end apart: 7, of which 7 were waited for; matrix products, arithmetic and copies ran while one was open for 4% of the time, Pallas kernels for 0%

commit v1 on v0

--- a/solution.py
+++ b/solution.py
@@ -11,7 +11,7 @@
 
 def broadcast(block, axis, source):
     block = jnp.where(lax.axis_index(axis) == source, block, jnp.zeros_like(block))
-    return lax.psum(block, axis)
+    return jnp.sum(lax.all_gather(block, axis), axis=0)
 
 
 def rms_norm(values, totals, gain):

time: 493 us -> 506 us (1.026)
  other arithmetic: 17.1 us -> 26.7 us
  waiting for transfers between devices: 365 us -> 372 us
    psum x1 -> x0, waiting for transfers between devices: 46.5 us -> none  [broadcast(): return lax.psum(block, axis)]
    all_gather x0 -> x2, waiting for transfers between devices: none -> 43.5 us  [broadcast(): return jnp.sum(lax.all_gather(block, axis), axis=0)]
    reduce_scatter x1, waiting for transfers between devices: 50 us -> 69.1 us  [local(): lax.psum_scatter(up_part, 'section', scatter_dimension=0, tiled=True)]
    reduce_scatter x1, waiting for transfers between devices: 69.1 us -> 50 us  [local(): lax.psum_scatter(gate_part, 'section', scatter_dimension=0, tiled=True)]
    all_gather x1, waiting for transfers between devices: 34.4 us -> 45 us  [local(): attn_rows = lax.all_gather(attn_input, 'sample', axis=0, tiled=True)]
    reduce_sum x0 -> x2, other arithmetic: none -> 8.78 us  [broadcast(): return jnp.sum(lax.all_gather(block, axis), axis=0)]
  transfers between devices with their start and end apart: 7 -> 8, of which waited for: 7 -> 8; matrix products, arithmetic and copies ran while one was open for 4% -> 7% of each run, Pallas kernels for 0% -> 0%
where the time goes in v1:
time: 506 us
  waiting for transfers between devices  372 us (74%)
  matrix products  57.6 us (11%)
  blocking collectives  31.5 us (6%)
  other arithmetic  26.7 us (5%)
  between operations  14.2 us (3%)
    reduce_scatter x1, waiting for transfers between devices, local(): lax.psum_scatter(jnp.dot(hidden_units, down_weight, preferred_element_typ...  86.8 us
    reduce_scatter x1, waiting for transfers between devices, local(): lax.psum_scatter(up_part, 'section', scatter_dimension=0, tiled=True)  69.1 us
    reduce_scatter x1, waiting for transfers between devices, local(): lax.psum_scatter(gate_part, 'section', scatter_dimension=0, tiled=True)  50 us
    all_gather x1, waiting for transfers between devices, local(): lax.all_gather((mlp_input, live_local), 'sample', axis=0, tiled=True)  46.1 us
    all_gather x1, waiting for transfers between devices, local(): attn_rows = lax.all_gather(attn_input, 'sample', axis=0, tiled=True)  45 us
    all_gather x2, waiting for transfers between devices, broadcast(): return jnp.sum(lax.all_gather(block, axis), axis=0)  43.5 us
    all_gather x1, waiting for transfers between devices, local(): hidden_units = lax.all_gather(share_units, 'section', axis=0, tiled=True)  31.6 us
    dot_general x2, matrix products, covariance(): lax.dot_general(weighted, columns, TOKEN_CONTRACT, preferred_element_type...  13.7 us
  transfers between devices with their start and end apart: 8, of which 8 were waited for; matrix products, arithmetic and copies ran while one was open for 7% of the time, Pallas kernels for 0%

profile of v1, /device:TPU:0, one launch (start us, length us, event | category | flops | bytes accessed | tf_op | source)
XLA Modules:
  0.0 505.8 jit_solution(8545747548678195092)
XLA Ops:
  7.2 0.0 all-gather.9.cloned.1.call-start
  7.2 0.7 convert_element_type.35
  7.9 1.2 multiply_reduce_fusion
  9.1 8.4 %psum.14 = f32[128]{0:T(128)S(1)} all-reduce(f32[128]{0:T(128)S(1)} %multiply_reduce_fusion), channel_id=1, replica_groups=mesh['sample'=4,'tensor'=2,'section'=4] {'section'}, use_global_device_ids=true, to_apply=%region_1.2 | all-reduce | flops 128 | bytes 1024 | tf_op jit(solution)/shard_map/psum | solution.py:42
  17.5 2.0 multiply_convert_fusion.1
  19.5 0.0 all-gather.9.cloned.1.call-update
  19.6 0.0 reduce-scatter.4.cloned.1.call-start
  19.6 46.1 %all-gather.9.cloned.1.call-done = bf16[512,2048]{1,0:T(8,128)(2,1)} async-done(((bf16[128,2048]{1,0:T(8,128)(2,1)}), bf16[512,2048]{1,0:T(8,128)(2,1)}) %all-gather.9.cloned.1.call-update) | async-done | bytes 2097168 | tf_op jit(solution)/shard_map/all_gather | solution.py:45
  65.7 13.5 %fusion.16 = f32[512,3584]{1,0:T(8,128)} fusion(bf16[512,2048]{1,0:T(8,128)(2,1)} %all-gather.9.cloned.1.call-done, bf16[3584,2048]{1,0:T(8,128)(2,1)} %param.11), kind=kOutput, calls=%fused_computation.34 | convolution fusion | flops 7516192768 | bytes 24117248 | tf_op jit(solution)/shard_map/dot_general | solution.py:46
  79.2 0.0 copy-start.1
  79.2 0.0 reduce-scatter.4.cloned.1.call-update
  79.2 0.0 reduce-scatter.6.cloned.1.call-start
  79.3 1.5 copy-done.1
  80.8 13.3 %fusion.17 = f32[512,3584]{1,0:T(8,128)} fusion(bf16[512,2048]{1,0:T(8,128)(2,1)S(1)} %copy-done.1, bf16[3584,2048]{1,0:T(8,128)(2,1)} %param.12), kind=kOutput, calls=%fused_computation.35 | convolution fusion | flops 7516192768 | bytes 24117248 | tf_op jit(solution)/shard_map/dot_general | solution.py:49
  94.1 0.0 reduce-scatter.6.cloned.1.call-update
  94.1 0.0 all-gather.11.cloned.1.call-start
  94.2 50.0 %reduce-scatter.4.cloned.1.call-done = f32[128,3584]{1,0:T(8,128)} async-done(((f32[512,3584]{1,0:T(8,128)}), f32[128,3584]{1,0:T(8,128)}) %reduce-scatter.4.cloned.1.call-update) | async-done | bytes 1835024 | tf_op jit(solution)/shard_map/reduce_scatter | solution.py:53
  144.2 69.1 %reduce-scatter.6.cloned.1.call-done = f32[128,3584]{1,0:T(8,128)} async-done(((f32[512,3584]{1,0:T(8,128)}), f32[128,3584]{1,0:T(8,128)}) %reduce-scatter.6.cloned.1.call-update) | async-done | bytes 1835024 | tf_op jit(solution)/shard_map/reduce_scatter | solution.py:54
  213.3 3.5 multiply_convert_fusion
  216.7 0.0 all-gather.11.cloned.1.call-update
  216.8 0.0 reduce-scatter.8.cloned.1.call-start
  216.8 31.6 %all-gather.11.cloned.1.call-done = bf16[512,3584]{1,0:T(8,128)(2,1)} async-done(((bf16[128,3584]{1,0:T(8,128)(2,1)}), bf16[512,3584]{1,0:T(8,128)(2,1)}) %all-gather.11.cloned.1.call-update) | async-done | bytes 3670032 | tf_op jit(solution)/shard_map/all_gather | solution.py:57
  248.4 13.4 %fusion.18 = f32[512,2048]{1,0:T(8,128)} fusion(bf16[512,3584]{1,0:T(8,128)(2,1)} %all-gather.11.cloned.1.call-done, bf16[3584,2048]{1,0:T(8,128)(2,1)} %param.13), kind=kOutput, calls=%fused_computation.36 | convolution fusion | flops 7516192768 | bytes 22544384 | tf_op jit(solution)/shard_map/dot_general | solution.py:60
  261.7 0.0 copy-start
  261.7 0.0 reduce-scatter.8.cloned.1.call-update
  261.8 0.0 all-gather.13.cloned.1.call-start
  261.8 1.0 copy-done
  262.8 1.1 convert_element_type.34
  263.9 0.0 copy-done.4
  263.9 86.8 %reduce-scatter.8.cloned.1.call-done = f32[64,2048]{1,0:T(8,128)} async-done(((f32[512,2048]{1,0:T(8,128)}), f32[64,2048]{1,0:T(8,128)}) %reduce-scatter.8.cloned.1.call-update) | async-done | bytes 524304 | tf_op jit(solution)/shard_map/reduce_scatter | solution.py:59
  350.6 1.3 add_convert_fusion
  351.9 8.3 %all_gather.29 = bf16[128,2048]{1,0:T(8,128)(2,1)S(1)} all-gather(bf16[64,2048]{1,0:T(8,128)(2,1)S(1)} %add_convert_fusion), channel_id=1, replica_groups=mesh['sample'=4,'tensor'=2,'section'=4] {'tensor'}, dimensions={0}, use_global_device_ids=true | all-gather | bytes 786432 | tf_op jit(solution)/shard_map/all_gather | solution.py:69
  360.2 0.2 fusion.2
  360.4 5.7 %psum.15 = f32[128]{0:T(128)S(1)} all-reduce(f32[128]{0:T(128)S(1)} %fusion.2), channel_id=1, replica_groups=mesh['sample'=4,'tensor'=2,'section'=4] {'section'}, use_global_device_ids=true, to_apply=%region_8.9 | all-reduce | flops 128 | bytes 1024 | tf_op jit(solution)/shard_map/psum | solution.py:71
  366.1 1.0 fusion.4
  367.0 0.0 all-gather.13.cloned.1.call-update
  367.1 0.0 all-gather.15.cloned.1.call-start
  367.1 1.2 dynamic-slice_select_fusion.1
  368.4 0.0 all-gather.15.cloned.1.call-update
  368.4 0.0 all-gather.17.cloned.1.call-start
  368.4 45.0 %all-gather.13.cloned.1.call-done = bf16[512,2048]{1,0:T(8,128)(2,1)} async-done(((bf16[128,2048]{1,0:T(8,128)(2,1)}), bf16[512,2048]{1,0:T(8,128)(2,1)}) %all-gather.13.cloned.1.call-update) | async-done | bytes 2097168 | tf_op jit(solution)/shard_map/all_gather | solution.py:76
  413.4 2.4 dynamic-slice_select_fusion
  415.8 0.0 all-gather.17.cloned.1.call-update
  415.8 0.0 copy-done.5
  415.9 9.1 %all-gather.2 = bf16[4,1,128]{2,1,0:T(2,128)(2,1)S(1)} all-gather(bf16[1,1,128]{2,1,0:T(2,128)(2,1)S(1)} %fusion.15), channel_id=1, replica_groups=mesh['sample'=4,'tensor'=2,'section'=4] {'sample'}, dimensions={0}, use_global_device_ids=true | all-gather | bytes 1280 | tf_op jit(solution)/shard_map/all_gather | solution.py:45
  425.0 0.6 convert_reduce_fusion
  425.6 0.4 fusion.13
  426.0 0.7 broadcast_divide_fusion.1
  426.7 22.2 %all-gather.15.cloned.1.call-done = bf16[2048,1024]{1,0:T(8,128)(2,1)} async-done(((bf16[512,1024]{1,0:T(8,128)(2,1)}), bf16[2048,1024]{1,0:T(8,128)(2,1)}) %all-gather.15.cloned.1.call-update) | async-done | bytes 4194320 | tf_op jit(solution)/shard_map/all_gather | solution.py:14
  448.8 4.4 reduce_sum.52
  453.2 1.5 fusion.11
  454.7 0.7 broadcast_divide_fusion.3
  455.3 0.0 copy-start.2
  455.4 7.0 %multiply_subtract_fusion.1 = f32[2048,1024]{1,0:T(8,128)} fusion(f32[1024]{0:T(1024)S(1)} %broadcast_divide_fusion.3, f32[2048]{0:T(1024)S(1)} %broadcast_divide_fusion.1, f32[]{:T(128)} %convert_reduce_fusion, bf16[512,1024]{1,0:T(8,128)(2,1)} %reduce_sum.52, bf16[512,2048]{1,0:T(8,128)(2,1)S(1)} %copy-done.1, bf16[512]{0:T(512)(128)(2,1)S(1)} %bitcast.37), kind=kOutput, calls=%fused_computation.1 | convolution fusion | flops 2154823680 | bytes 11547652 | tf_op jit(solution)/shard_map/dot_general | solution.py:24
  462.4 0.0 copy-done.2
  462.4 0.4 fusion.9
  462.7 0.8 broadcast_divide_fusion
  463.6 21.3 %all-gather.17.cloned.1.call-done = bf16[2048,1024]{1,0:T(8,128)(2,1)} async-done(((bf16[512,1024]{1,0:T(8,128)(2,1)}), bf16[2048,1024]{1,0:T(8,128)(2,1)}) %all-gather.17.cloned.1.call-update) | async-done | bytes 4194320 | tf_op jit(solution)/shard_map/all_gather | solution.py:14
  484.9 4.4 reduce_sum.55
  489.3 1.5 fusion.7
  490.7 0.7 broadcast_divide_fusion.2
  491.4 0.0 copy-done.3
  491.4 6.7 %multiply_subtract_fusion = f32[2048,1024]{1,0:T(8,128)} fusion(f32[1024]{0:T(1024)S(1)} %broadcast_divide_fusion.2, f32[2048]{0:T(1024)S(1)} %broadcast_divide_fusion, f32[]{:T(128)} %convert_reduce_fusion, bf16[512,1024]{1,0:T(8,128)(2,1)} %reduce_sum.55, bf16[512,2048]{1,0:T(8,128)(2,1)S(1)} %copy-done.3, bf16[512]{0:T(512)(128)(2,1)S(1)} %bitcast.38), kind=kOutput, calls=%fused_computation | convolution fusion | flops 2154823680 | bytes 11547652 | tf_op jit(solution)/shard_map/dot_general | solution.py:24
  498.1 0.8 copy.11
  (8 shorter events, 0.0 us)
Async XLA Ops:
  7.2 58.5 %all-gather.9.cloned.1.call-start = ((), (), s32[]{:S(2)}) async-start(), calls=%async_computation.3 | async-start | bytes 2621440 | tf_op jit(solution)/shard_map/all_gather | solution.py:45
  19.6 124.6 %reduce-scatter.4.cloned.1.call-start = ((), (), s32[]{:S(2)}) async-start(), calls=%async_computation.4 | async-start | bytes 9175040 | tf_op jit(solution)/shard_map/reduce_scatter | solution.py:53
  79.2 1.6 copy-start.1
  79.2 134.0 %reduce-scatter.6.cloned.1.call-start = ((), (), s32[]{:S(2)}) async-start(), calls=%async_computation.5 | async-start | bytes 9175040 | tf_op jit(solution)/shard_map/reduce_scatter | solution.py:54
  94.1 154.3 %all-gather.11.cloned.1.call-start = ((), (), s32[]{:S(2)}) async-start(), calls=%async_computation.6 | async-start | bytes 4587520 | tf_op jit(solution)/shard_map/all_gather | solution.py:57
  216.8 133.9 %reduce-scatter.8.cloned.1.call-start = ((), (), s32[]{:S(2)}) async-start(), calls=%async_computation.7 | async-start | bytes 4718592 | tf_op jit(solution)/shard_map/reduce_scatter | solution.py:59
  261.7 1.0 copy-start
  261.7 2.1 copy-start.4
  261.8 151.6 %all-gather.13.cloned.1.call-start = ((), (), s32[]{:S(2)}) async-start(), calls=%async_computation.8 | async-start | bytes 2621440 | tf_op jit(solution)/shard_map/all_gather | solution.py:76
  367.0 48.8 %copy-start.5 = (s32[128]{0:T(128)S(1)}, s32[128]{0:T(128)}, u32[]{:S(2)}) copy-start(s32[128]{0:T(128)} %param.8) | copy-start | bytes 1540
  367.1 81.8 %all-gather.15.cloned.1.call-start = ((), (), s32[]{:S(2)}) async-start(), calls=%async_computation.9 | async-start | bytes 5242880 | tf_op jit(solution)/shard_map/all_gather | solution.py:14
  368.4 116.5 %all-gather.17.cloned.1.call-start = ((), (), s32[]{:S(2)}) async-start(), calls=%async_computation.10 | async-start | bytes 5242880 | tf_op jit(solution)/shard_map/all_gather | solution.py:14
  455.3 7.0 %copy-start.2 = (bf16[512,2048]{1,0:T(8,128)(2,1)S(1)}, bf16[512,2048]{1,0:T(8,128)(2,1)}, u32[]{:S(2)}) copy-start(bf16[512,2048]{1,0:T(8,128)(2,1)} %all-gather.13.cloned.1.call-done) | copy-start | bytes 6291460
  462.7 28.7 %copy-start.3 = (bf16[512,2048]{1,0:T(8,128)(2,1)S(1)}, bf16[512,2048]{1,0:T(8,128)(2,1)}, u32[]{:S(2)}) copy-start(bf16[512,2048]{1,0:T(8,128)(2,1)} %all-gather.13.cloned.1.call-done) | copy-start | bytes 6291460
Sparse Core Ops, SparseCore 0:
  19.7 45.9 all-gather.8
  79.4 64.7 reduce-scatter.3
  147.3 65.9 reduce-scatter.5
  216.9 31.4 all-gather.10
  261.9 88.6 reduce-scatter.7
  367.2 46.1 all-gather.12
  415.5 33.2 all-gather.14
  450.4 34.4 all-gather.16
